TPU v7x, 256 devices: a whole 4x4x8 slice. The times are simulated.
256 devices in a mesh: tile: 64 (over y, z, core), sec: 4 (over x).
Axes of the slice: x: 4, y: 4, z: 8, core: 2. Of those that a mesh axis runs over, the one named last changes fastest.
Arguments:
- voltage: float32 [8192, 512], P('tile', 'sec'), may hold values from -6 to 6
- conductance: float32 [8192, 512], P('tile', 'sec'), may hold values from 0.2 to 2
- reversal: float32 [8192, 512], P('tile', 'sec'), may hold values from -1 to 1
- drive: bfloat16 [8, 8192, 512], P(None, 'tile', 'sec'), may hold values from -6 to 6
- inv_cable: float32 [128, 128], replicated, may hold values from -1 to 1
- owner_map: int32 [8192], P('tile'), may hold values from 0 to 63, as said below
- peer_counts: int32 [64, 64], P('tile'), may hold values from 0 to 4, as said below
- pattern: int32 [4, 8192, 2], P('sec', 'tile'), may hold values from 0 to 31, all different within a row
- transfer: bfloat16 [4, 8192, 2, 128, 128], P('sec', 'tile'), may hold values from -0.01171875 to 0.01171875
Outputs:
- final_voltage: float32 [8192, 512], P('tile', 'sec')
- probe: float32 [8, 4096], P(None, ('tile', 'sec'))
Inputs may be any that keep to these rules, and one draw needn't show every extreme that they name: `owner_map`: every depth tile owns exactly 128 cells; the cells c with c // 128 = u include at most 4 cells of one owner, and exactly 4 of some owner. peer_counts[d, u] is the number of cells c with c // 128 = u and owner_map[c] = d. `pattern`: the 2 contact tiles of one slot and section differ.
All inputs are finite; a program needn't handle non-finite values.
Results may differ from a plain program's by a relative error of at most 0.0029.
Values may be sent and summed in bfloat16 or wider, within the bound.
A program may use at most 64 MiB of HBM per device.

v0:
```python
import jax
import jax.numpy as jnp
from jax import lax
from jax.sharding import PartitionSpec as P

CONTACTS = 4096
TIME_STEP = 0.25
AXIAL = 2.0


def padded_2(block, sides, width):
    for axis, dim in sides:
        count = lax.axis_size(axis)
        forward = [(i, i + 1) for i in range(count - 1)]
        backward = [(target, source) for source, target in forward]
        low = lax.ppermute(
            lax.slice_in_dim(block, block.shape[dim] - width, None, axis=dim), axis, forward
        )
        high = lax.ppermute(lax.slice_in_dim(block, 0, width, axis=dim), axis, backward)
        block = jnp.concatenate([low, block, high], axis=dim)
    return block


def cable_update(voltage_now, conductance, reversal, drive_now, inv_cable):
    padded = padded_2(voltage_now.astype(jnp.bfloat16), (("sec", 1),), 1).astype(voltage_now.dtype)
    columns = jnp.arange(voltage_now.shape[1], dtype=jnp.int32)
    first_col = (columns == 0).astype(jnp.float32)
    last_col = (columns == voltage_now.shape[1] - 1).astype(jnp.float32)
    boundary = first_col * (padded[:, :-2] - voltage_now) + last_col * (padded[:, 2:] - voltage_now)
    driven = drive_now.astype(jnp.float32)
    right_side = voltage_now * (1.0 - TIME_STEP * conductance) + TIME_STEP * (
        conductance * reversal + driven + AXIAL * boundary
    )
    voltage_next = jnp.einsum("ci,ji->cj", right_side, inv_cable, precision=lax.Precision.HIGHEST)
    current = (conductance * (voltage_next - reversal) - driven).astype(jnp.bfloat16)
    return (voltage_next, current)


def on_device(
    voltage, conductance, reversal, drive, inv_cable, owner_map, peer_counts, pattern, transfer
):
    cell_count = voltage.shape[0]
    seg_width = voltage.shape[1]
    step_count = drive.shape[0]
    tile_count = lax.axis_size("tile")
    section_count = lax.axis_size("sec")
    capacity = 2 * cell_count // tile_count
    owners = jnp.arange(tile_count, dtype=jnp.int32)
    member = (owner_map[:, None] == owners[None, :]).astype(jnp.int32)
    rank_within = jnp.sum(jnp.cumsum(member, axis=0) * member, axis=1) - 1
    placed = owner_map * capacity + rank_within
    source_row = (
        jnp.full((tile_count * capacity,), cell_count, jnp.int32)
        .at[placed]
        .set(jnp.arange(cell_count, dtype=jnp.int32))
    )
    blank_row = jnp.zeros((1, seg_width), jnp.bfloat16)

    def advance_send(voltage_now, drive_now):
        voltage_next, current = cable_update(
            voltage_now, conductance, reversal, drive_now, inv_cable
        )
        outgoing = jnp.take(jnp.concatenate([current, blank_row], axis=0), source_row, axis=0)
        outgoing = outgoing.reshape(tile_count, capacity, seg_width)
        arrived = lax.all_to_all(outgoing, "tile", split_axis=0, concat_axis=0, tiled=True)
        return (voltage_next, arrived)

    final_voltage, arrived = lax.scan(advance_send, voltage, drive)
    received = arrived.reshape(step_count, tile_count * capacity, seg_width)
    counts = peer_counts[0]
    end_rows = jnp.cumsum(counts)
    starts = end_rows - counts
    slot_ids = jnp.arange(cell_count, dtype=jnp.int32)
    source = jnp.sum((end_rows[None, :] <= slot_ids[:, None]).astype(jnp.int32), axis=1)
    offset = jnp.sum(jnp.where(source[:, None] == owners[None, :], starts[None, :], 0), axis=1)
    gather_rows = source * capacity + slot_ids - offset
    ordered = jnp.take(received, gather_rows, axis=1)
    weights = transfer[0]
    layout = pattern[0]
    contact_width = weights.shape[3]
    tile_total = CONTACTS // contact_width
    tile_sums = jnp.einsum("tsi,skic->tskc", ordered, weights, preferred_element_type=jnp.float32)
    select = (layout[:, :, None] == jnp.arange(tile_total, dtype=jnp.int32)[None, None, :]).astype(
        jnp.float32
    )
    partial_sum = jnp.einsum("tskc,skq->tqc", tile_sums, select, precision=lax.Precision.HIGHEST)
    partial_sum = partial_sum.reshape(step_count, tile_total * contact_width)
    summed = lax.psum(partial_sum, ("tile", "sec"))
    share_width = summed.shape[1] // (tile_count * section_count)
    position = lax.axis_index("tile") * section_count + lax.axis_index("sec")
    probe_share = lax.dynamic_slice_in_dim(summed, position * share_width, share_width, 1)
    return (final_voltage, probe_share)


def solution(mesh):
    placed = (
        P("tile", "sec"),
        P("tile", "sec"),
        P("tile", "sec"),
        P(None, "tile", "sec"),
        P(),
        P("tile"),
        P("tile", None),
        P("sec", "tile", None),
        P("sec", "tile", None, None, None),
    )
    return jax.shard_map(
        on_device,
        mesh=mesh,
        in_specs=placed,
        out_specs=(P("tile", "sec"), P(None, ("tile", "sec"))),
        check_vma=False,
    )
```

profile of v0, /device:TPU:8, one launch (start us, length us, event | category | flops | bytes accessed | tf_op | source)
XLA Modules:
  0.0 478.0 jit_solution(9085325909894427495)
XLA Ops:
  14.3 208.3 %while.13 = (s32[]{:T(128)}, f32[128,128]{1,0:T(8,128)S(1)}, bf16[8,64,4,128]{3,2,1,0:T(4,128)(2,1)S(1)}, f32[128,128]{1,0:T(8,128)}, bf16[8,128,128]{2,1,0:T(8,...) while((s32[]{:T(128)}, f32[128,128]{1,0:T(8,128)S(1)}, ...), condition=%wide.region_4.5_spmd, body=%wide.region_3.4_spmd.sunk | while | flops 25629952 | bytes 1626603 | solution.py:68
  14.4 1.3 collective-permute-start
  15.7 4.5 collective-permute-start.1
  20.4 1.4 collective-permute-done.1
  21.9 1.3 fusion.52
  24.8 12.1 %all-to-all-start = ((bf16[64,4,128]{2,1,0:T(4,128)(2,1)}), bf16[64,4,128]{2,1,0:T(4,128)(2,1)S(1)}, u32[]{:S(2)}, u32[]{:S(2)}) async-start(bf16[64,4,128]{2,1,0:T(4,128)(2,1)} %broadcast_select_fusion.2), calls=%async_computation | async-start | bytes 131072 | tf_op jit(solution)/shard_map/while/body/eval_jaxpr/all_to_all | solution.py:65
  36.9 8.8 %all-to-all-done = bf16[64,4,128]{2,1,0:T(4,128)(2,1)S(1)} async-done(((bf16[64,4,128]{2,1,0:T(4,128)(2,1)}), bf16[64,4,128]{2,1,0:T(4,128)(2,1)S(1)}, u32[]{:S(2)}, u32[]{:S(2)}) %all-to-all-start) | async-done | bytes 65568 | tf_op jit(solution)/shard_map/while/body/eval_jaxpr/all_to_all | solution.py:65
  45.9 1.3 collective-permute-start
  47.2 4.9 %collective-permute-start.1 = (bf16[128,1]{1,0:T(8,128)(2,1)S(1)}, bf16[128,1]{1,0:T(8,128)(2,1)S(1)}, u32[]{:S(2)}, u32[]{:S(2)}) collective-permute-start(bf16[128,1]{1,0:T(8,128)(2,1)S(1)} %get-tuple-element.171), channel_id=1, source_target_pairs={{0,1},{1,2},{2,3},{4,5},{5,6},{6,7},{8,9},{9,10},{10,11},{12,13},{... | collective-permute-start | bytes 776 | tf_op jit(solution)/shard_map/while/body/eval_jaxpr/ppermute | solution.py:16
  52.2 1.4 collective-permute-done.1
  53.7 1.3 fusion.52
  56.7 5.5 %all-to-all-start = ((bf16[64,4,128]{2,1,0:T(4,128)(2,1)}), bf16[64,4,128]{2,1,0:T(4,128)(2,1)S(1)}, u32[]{:S(2)}, u32[]{:S(2)}) async-start(bf16[64,4,128]{2,1,0:T(4,128)(2,1)} %broadcast_select_fusion.2), calls=%async_computation | async-start | bytes 131072 | tf_op jit(solution)/shard_map/while/body/eval_jaxpr/all_to_all | solution.py:65
  62.2 8.8 %all-to-all-done = bf16[64,4,128]{2,1,0:T(4,128)(2,1)S(1)} async-done(((bf16[64,4,128]{2,1,0:T(4,128)(2,1)}), bf16[64,4,128]{2,1,0:T(4,128)(2,1)S(1)}, u32[]{:S(2)}, u32[]{:S(2)}) %all-to-all-start) | async-done | bytes 65568 | tf_op jit(solution)/shard_map/while/body/eval_jaxpr/all_to_all | solution.py:65
  71.2 1.3 collective-permute-start
  72.5 4.9 %collective-permute-start.1 = (bf16[128,1]{1,0:T(8,128)(2,1)S(1)}, bf16[128,1]{1,0:T(8,128)(2,1)S(1)}, u32[]{:S(2)}, u32[]{:S(2)}) collective-permute-start(bf16[128,1]{1,0:T(8,128)(2,1)S(1)} %get-tuple-element.171), channel_id=1, source_target_pairs={{0,1},{1,2},{2,3},{4,5},{5,6},{6,7},{8,9},{9,10},{10,11},{12,13},{... | collective-permute-start | bytes 776 | tf_op jit(solution)/shard_map/while/body/eval_jaxpr/ppermute | solution.py:16
  77.5 1.4 collective-permute-done.1
  79.0 1.3 fusion.52
  81.9 5.5 %all-to-all-start = ((bf16[64,4,128]{2,1,0:T(4,128)(2,1)}), bf16[64,4,128]{2,1,0:T(4,128)(2,1)S(1)}, u32[]{:S(2)}, u32[]{:S(2)}) async-start(bf16[64,4,128]{2,1,0:T(4,128)(2,1)} %broadcast_select_fusion.2), calls=%async_computation | async-start | bytes 131072 | tf_op jit(solution)/shard_map/while/body/eval_jaxpr/all_to_all | solution.py:65
  87.4 8.8 %all-to-all-done = bf16[64,4,128]{2,1,0:T(4,128)(2,1)S(1)} async-done(((bf16[64,4,128]{2,1,0:T(4,128)(2,1)}), bf16[64,4,128]{2,1,0:T(4,128)(2,1)S(1)}, u32[]{:S(2)}, u32[]{:S(2)}) %all-to-all-start) | async-done | bytes 65568 | tf_op jit(solution)/shard_map/while/body/eval_jaxpr/all_to_all | solution.py:65
  96.4 1.3 collective-permute-start
  97.7 4.9 %collective-permute-start.1 = (bf16[128,1]{1,0:T(8,128)(2,1)S(1)}, bf16[128,1]{1,0:T(8,128)(2,1)S(1)}, u32[]{:S(2)}, u32[]{:S(2)}) collective-permute-start(bf16[128,1]{1,0:T(8,128)(2,1)S(1)} %get-tuple-element.171), channel_id=1, source_target_pairs={{0,1},{1,2},{2,3},{4,5},{5,6},{6,7},{8,9},{9,10},{10,11},{12,13},{... | collective-permute-start | bytes 776 | tf_op jit(solution)/shard_map/while/body/eval_jaxpr/ppermute | solution.py:16
  102.8 1.4 collective-permute-done.1
  107.2 5.5 %all-to-all-start = ((bf16[64,4,128]{2,1,0:T(4,128)(2,1)}), bf16[64,4,128]{2,1,0:T(4,128)(2,1)S(1)}, u32[]{:S(2)}, u32[]{:S(2)}) async-start(bf16[64,4,128]{2,1,0:T(4,128)(2,1)} %broadcast_select_fusion.2), calls=%async_computation | async-start | bytes 131072 | tf_op jit(solution)/shard_map/while/body/eval_jaxpr/all_to_all | solution.py:65
  112.7 8.8 %all-to-all-done = bf16[64,4,128]{2,1,0:T(4,128)(2,1)S(1)} async-done(((bf16[64,4,128]{2,1,0:T(4,128)(2,1)}), bf16[64,4,128]{2,1,0:T(4,128)(2,1)S(1)}, u32[]{:S(2)}, u32[]{:S(2)}) %all-to-all-start) | async-done | bytes 65568 | tf_op jit(solution)/shard_map/while/body/eval_jaxpr/all_to_all | solution.py:65
  121.7 1.3 collective-permute-start
  123.0 4.9 %collective-permute-start.1 = (bf16[128,1]{1,0:T(8,128)(2,1)S(1)}, bf16[128,1]{1,0:T(8,128)(2,1)S(1)}, u32[]{:S(2)}, u32[]{:S(2)}) collective-permute-start(bf16[128,1]{1,0:T(8,128)(2,1)S(1)} %get-tuple-element.171), channel_id=1, source_target_pairs={{0,1},{1,2},{2,3},{4,5},{5,6},{6,7},{8,9},{9,10},{10,11},{12,13},{... | collective-permute-start | bytes 776 | tf_op jit(solution)/shard_map/while/body/eval_jaxpr/ppermute | solution.py:16
  128.0 1.4 collective-permute-done.1
  132.4 5.5 %all-to-all-start = ((bf16[64,4,128]{2,1,0:T(4,128)(2,1)}), bf16[64,4,128]{2,1,0:T(4,128)(2,1)S(1)}, u32[]{:S(2)}, u32[]{:S(2)}) async-start(bf16[64,4,128]{2,1,0:T(4,128)(2,1)} %broadcast_select_fusion.2), calls=%async_computation | async-start | bytes 131072 | tf_op jit(solution)/shard_map/while/body/eval_jaxpr/all_to_all | solution.py:65
  137.9 8.8 %all-to-all-done = bf16[64,4,128]{2,1,0:T(4,128)(2,1)S(1)} async-done(((bf16[64,4,128]{2,1,0:T(4,128)(2,1)}), bf16[64,4,128]{2,1,0:T(4,128)(2,1)S(1)}, u32[]{:S(2)}, u32[]{:S(2)}) %all-to-all-start) | async-done | bytes 65568 | tf_op jit(solution)/shard_map/while/body/eval_jaxpr/all_to_all | solution.py:65
  146.9 1.3 collective-permute-start
  148.2 4.9 %collective-permute-start.1 = (bf16[128,1]{1,0:T(8,128)(2,1)S(1)}, bf16[128,1]{1,0:T(8,128)(2,1)S(1)}, u32[]{:S(2)}, u32[]{:S(2)}) collective-permute-start(bf16[128,1]{1,0:T(8,128)(2,1)S(1)} %get-tuple-element.171), channel_id=1, source_target_pairs={{0,1},{1,2},{2,3},{4,5},{5,6},{6,7},{8,9},{9,10},{10,11},{12,13},{... | collective-permute-start | bytes 776 | tf_op jit(solution)/shard_map/while/body/eval_jaxpr/ppermute | solution.py:16
  153.3 1.4 collective-permute-done.1
  154.8 1.3 fusion.52
  157.7 5.5 %all-to-all-start = ((bf16[64,4,128]{2,1,0:T(4,128)(2,1)}), bf16[64,4,128]{2,1,0:T(4,128)(2,1)S(1)}, u32[]{:S(2)}, u32[]{:S(2)}) async-start(bf16[64,4,128]{2,1,0:T(4,128)(2,1)} %broadcast_select_fusion.2), calls=%async_computation | async-start | bytes 131072 | tf_op jit(solution)/shard_map/while/body/eval_jaxpr/all_to_all | solution.py:65
  163.2 8.8 %all-to-all-done = bf16[64,4,128]{2,1,0:T(4,128)(2,1)S(1)} async-done(((bf16[64,4,128]{2,1,0:T(4,128)(2,1)}), bf16[64,4,128]{2,1,0:T(4,128)(2,1)S(1)}, u32[]{:S(2)}, u32[]{:S(2)}) %all-to-all-start) | async-done | bytes 65568 | tf_op jit(solution)/shard_map/while/body/eval_jaxpr/all_to_all | solution.py:65
  172.2 1.3 collective-permute-start
  173.5 4.9 %collective-permute-start.1 = (bf16[128,1]{1,0:T(8,128)(2,1)S(1)}, bf16[128,1]{1,0:T(8,128)(2,1)S(1)}, u32[]{:S(2)}, u32[]{:S(2)}) collective-permute-start(bf16[128,1]{1,0:T(8,128)(2,1)S(1)} %get-tuple-element.171), channel_id=1, source_target_pairs={{0,1},{1,2},{2,3},{4,5},{5,6},{6,7},{8,9},{9,10},{10,11},{12,13},{... | collective-permute-start | bytes 776 | tf_op jit(solution)/shard_map/while/body/eval_jaxpr/ppermute | solution.py:16
  178.5 1.4 collective-permute-done.1
  182.9 5.5 %all-to-all-start = ((bf16[64,4,128]{2,1,0:T(4,128)(2,1)}), bf16[64,4,128]{2,1,0:T(4,128)(2,1)S(1)}, u32[]{:S(2)}, u32[]{:S(2)}) async-start(bf16[64,4,128]{2,1,0:T(4,128)(2,1)} %broadcast_select_fusion.2), calls=%async_computation | async-start | bytes 131072 | tf_op jit(solution)/shard_map/while/body/eval_jaxpr/all_to_all | solution.py:65
  188.5 8.8 %all-to-all-done = bf16[64,4,128]{2,1,0:T(4,128)(2,1)S(1)} async-done(((bf16[64,4,128]{2,1,0:T(4,128)(2,1)}), bf16[64,4,128]{2,1,0:T(4,128)(2,1)S(1)}, u32[]{:S(2)}, u32[]{:S(2)}) %all-to-all-start) | async-done | bytes 65568 | tf_op jit(solution)/shard_map/while/body/eval_jaxpr/all_to_all | solution.py:65
  197.5 1.3 collective-permute-start
  198.7 4.9 %collective-permute-start.1 = (bf16[128,1]{1,0:T(8,128)(2,1)S(1)}, bf16[128,1]{1,0:T(8,128)(2,1)S(1)}, u32[]{:S(2)}, u32[]{:S(2)}) collective-permute-start(bf16[128,1]{1,0:T(8,128)(2,1)S(1)} %get-tuple-element.171), channel_id=1, source_target_pairs={{0,1},{1,2},{2,3},{4,5},{5,6},{6,7},{8,9},{9,10},{10,11},{12,13},{... | collective-permute-start | bytes 776 | tf_op jit(solution)/shard_map/while/body/eval_jaxpr/ppermute | solution.py:16
  203.8 1.4 collective-permute-done.1
  208.2 5.5 %all-to-all-start = ((bf16[64,4,128]{2,1,0:T(4,128)(2,1)}), bf16[64,4,128]{2,1,0:T(4,128)(2,1)S(1)}, u32[]{:S(2)}, u32[]{:S(2)}) async-start(bf16[64,4,128]{2,1,0:T(4,128)(2,1)} %broadcast_select_fusion.2), calls=%async_computation | async-start | bytes 131072 | tf_op jit(solution)/shard_map/while/body/eval_jaxpr/all_to_all | solution.py:65
  213.7 8.8 %all-to-all-done = bf16[64,4,128]{2,1,0:T(4,128)(2,1)S(1)} async-done(((bf16[64,4,128]{2,1,0:T(4,128)(2,1)}), bf16[64,4,128]{2,1,0:T(4,128)(2,1)S(1)}, u32[]{:S(2)}, u32[]{:S(2)}) %all-to-all-start) | async-done | bytes 65568 | tf_op jit(solution)/shard_map/while/body/eval_jaxpr/all_to_all | solution.py:65
  223.9 4.6 fusion.28
  230.1 239.7 %all-reduce.3.cloned.1.call-done = f32[8,4096]{1,0:T(8,128)} async-done(((f32[8,4096]{1,0:T(8,128)}), f32[8,4096]{1,0:T(8,128)}) %all-reduce.3.cloned.1.call-update) | async-done | bytes 131088 | tf_op jit(solution)/shard_map/psum | solution.py:88
  469.8 1.3 constant_dynamic-slice_fusion
  (144 shorter events, 30.9 us)
Async XLA Ops:
  7.2 462.6 %all-reduce.3.cloned.1.call-start = ((), (), s32[]{:S(2)}) async-start(), calls=%async_computation.1 | async-start | bytes 262144 | tf_op jit(solution)/shard_map/psum | solution.py:88
  14.4 6.0 %collective-permute-start = (bf16[128,1]{1,0:T(8,128)(2,1)S(1)}, bf16[128,1]{1,0:T(8,128)(2,1)S(1)}, u32[]{:S(2)}, u32[]{:S(2)}) collective-permute-start(bf16[128,1]{1,0:T(8,128)(2,1)S(1)} %get-tuple-element.170), channel_id=1, source_target_pairs={{1,0},{2,1},{3,2},{5,4},{6,5},{7,6},{9,8},{10,9},{11,10},{13,12},{... | collective-permute-start | bytes 776 | tf_op jit(solution)/shard_map/while/body/eval_jaxpr/ppermute | solution.py:19
  15.7 6.1 %collective-permute-start.1 = (bf16[128,1]{1,0:T(8,128)(2,1)S(1)}, bf16[128,1]{1,0:T(8,128)(2,1)S(1)}, u32[]{:S(2)}, u32[]{:S(2)}) collective-permute-start(bf16[128,1]{1,0:T(8,128)(2,1)S(1)} %get-tuple-element.171), channel_id=1, source_target_pairs={{0,1},{1,2},{2,3},{4,5},{5,6},{6,7},{8,9},{9,10},{10,11},{12,13},{... | collective-permute-start | bytes 776 | tf_op jit(solution)/shard_map/while/body/eval_jaxpr/ppermute | solution.py:16
  24.8 20.9 %all-to-all-start = ((bf16[64,4,128]{2,1,0:T(4,128)(2,1)}), bf16[64,4,128]{2,1,0:T(4,128)(2,1)S(1)}, u32[]{:S(2)}, u32[]{:S(2)}) async-start(bf16[64,4,128]{2,1,0:T(4,128)(2,1)} %broadcast_select_fusion.2), calls=%async_computation | async-start | bytes 131072 | tf_op jit(solution)/shard_map/while/body/eval_jaxpr/all_to_all | solution.py:65
  45.9 6.3 %collective-permute-start = (bf16[128,1]{1,0:T(8,128)(2,1)S(1)}, bf16[128,1]{1,0:T(8,128)(2,1)S(1)}, u32[]{:S(2)}, u32[]{:S(2)}) collective-permute-start(bf16[128,1]{1,0:T(8,128)(2,1)S(1)} %get-tuple-element.170), channel_id=1, source_target_pairs={{1,0},{2,1},{3,2},{5,4},{6,5},{7,6},{9,8},{10,9},{11,10},{13,12},{... | collective-permute-start | bytes 776 | tf_op jit(solution)/shard_map/while/body/eval_jaxpr/ppermute | solution.py:19
  47.2 6.4 %collective-permute-start.1 = (bf16[128,1]{1,0:T(8,128)(2,1)S(1)}, bf16[128,1]{1,0:T(8,128)(2,1)S(1)}, u32[]{:S(2)}, u32[]{:S(2)}) collective-permute-start(bf16[128,1]{1,0:T(8,128)(2,1)S(1)} %get-tuple-element.171), channel_id=1, source_target_pairs={{0,1},{1,2},{2,3},{4,5},{5,6},{6,7},{8,9},{9,10},{10,11},{12,13},{... | collective-permute-start | bytes 776 | tf_op jit(solution)/shard_map/while/body/eval_jaxpr/ppermute | solution.py:16
  56.7 14.4 %all-to-all-start = ((bf16[64,4,128]{2,1,0:T(4,128)(2,1)}), bf16[64,4,128]{2,1,0:T(4,128)(2,1)S(1)}, u32[]{:S(2)}, u32[]{:S(2)}) async-start(bf16[64,4,128]{2,1,0:T(4,128)(2,1)} %broadcast_select_fusion.2), calls=%async_computation | async-start | bytes 131072 | tf_op jit(solution)/shard_map/while/body/eval_jaxpr/all_to_all | solution.py:65
  71.2 6.3 %collective-permute-start = (bf16[128,1]{1,0:T(8,128)(2,1)S(1)}, bf16[128,1]{1,0:T(8,128)(2,1)S(1)}, u32[]{:S(2)}, u32[]{:S(2)}) collective-permute-start(bf16[128,1]{1,0:T(8,128)(2,1)S(1)} %get-tuple-element.170), channel_id=1, source_target_pairs={{1,0},{2,1},{3,2},{5,4},{6,5},{7,6},{9,8},{10,9},{11,10},{13,12},{... | collective-permute-start | bytes 776 | tf_op jit(solution)/shard_map/while/body/eval_jaxpr/ppermute | solution.py:19
  72.5 6.4 %collective-permute-start.1 = (bf16[128,1]{1,0:T(8,128)(2,1)S(1)}, bf16[128,1]{1,0:T(8,128)(2,1)S(1)}, u32[]{:S(2)}, u32[]{:S(2)}) collective-permute-start(bf16[128,1]{1,0:T(8,128)(2,1)S(1)} %get-tuple-element.171), channel_id=1, source_target_pairs={{0,1},{1,2},{2,3},{4,5},{5,6},{6,7},{8,9},{9,10},{10,11},{12,13},{... | collective-permute-start | bytes 776 | tf_op jit(solution)/shard_map/while/body/eval_jaxpr/ppermute | solution.py:16
  81.9 14.4 %all-to-all-start = ((bf16[64,4,128]{2,1,0:T(4,128)(2,1)}), bf16[64,4,128]{2,1,0:T(4,128)(2,1)S(1)}, u32[]{:S(2)}, u32[]{:S(2)}) async-start(bf16[64,4,128]{2,1,0:T(4,128)(2,1)} %broadcast_select_fusion.2), calls=%async_computation | async-start | bytes 131072 | tf_op jit(solution)/shard_map/while/body/eval_jaxpr/all_to_all | solution.py:65
  96.4 6.3 %collective-permute-start = (bf16[128,1]{1,0:T(8,128)(2,1)S(1)}, bf16[128,1]{1,0:T(8,128)(2,1)S(1)}, u32[]{:S(2)}, u32[]{:S(2)}) collective-permute-start(bf16[128,1]{1,0:T(8,128)(2,1)S(1)} %get-tuple-element.170), channel_id=1, source_target_pairs={{1,0},{2,1},{3,2},{5,4},{6,5},{7,6},{9,8},{10,9},{11,10},{13,12},{... | collective-permute-start | bytes 776 | tf_op jit(solution)/shard_map/while/body/eval_jaxpr/ppermute | solution.py:19
  97.7 6.4 %collective-permute-start.1 = (bf16[128,1]{1,0:T(8,128)(2,1)S(1)}, bf16[128,1]{1,0:T(8,128)(2,1)S(1)}, u32[]{:S(2)}, u32[]{:S(2)}) collective-permute-start(bf16[128,1]{1,0:T(8,128)(2,1)S(1)} %get-tuple-element.171), channel_id=1, source_target_pairs={{0,1},{1,2},{2,3},{4,5},{5,6},{6,7},{8,9},{9,10},{10,11},{12,13},{... | collective-permute-start | bytes 776 | tf_op jit(solution)/shard_map/while/body/eval_jaxpr/ppermute | solution.py:16
  107.2 14.4 %all-to-all-start = ((bf16[64,4,128]{2,1,0:T(4,128)(2,1)}), bf16[64,4,128]{2,1,0:T(4,128)(2,1)S(1)}, u32[]{:S(2)}, u32[]{:S(2)}) async-start(bf16[64,4,128]{2,1,0:T(4,128)(2,1)} %broadcast_select_fusion.2), calls=%async_computation | async-start | bytes 131072 | tf_op jit(solution)/shard_map/while/body/eval_jaxpr/all_to_all | solution.py:65
  121.7 6.3 %collective-permute-start = (bf16[128,1]{1,0:T(8,128)(2,1)S(1)}, bf16[128,1]{1,0:T(8,128)(2,1)S(1)}, u32[]{:S(2)}, u32[]{:S(2)}) collective-permute-start(bf16[128,1]{1,0:T(8,128)(2,1)S(1)} %get-tuple-element.170), channel_id=1, source_target_pairs={{1,0},{2,1},{3,2},{5,4},{6,5},{7,6},{9,8},{10,9},{11,10},{13,12},{... | collective-permute-start | bytes 776 | tf_op jit(solution)/shard_map/while/body/eval_jaxpr/ppermute | solution.py:19
  123.0 6.4 %collective-permute-start.1 = (bf16[128,1]{1,0:T(8,128)(2,1)S(1)}, bf16[128,1]{1,0:T(8,128)(2,1)S(1)}, u32[]{:S(2)}, u32[]{:S(2)}) collective-permute-start(bf16[128,1]{1,0:T(8,128)(2,1)S(1)} %get-tuple-element.171), channel_id=1, source_target_pairs={{0,1},{1,2},{2,3},{4,5},{5,6},{6,7},{8,9},{9,10},{10,11},{12,13},{... | collective-permute-start | bytes 776 | tf_op jit(solution)/shard_map/while/body/eval_jaxpr/ppermute | solution.py:16
  132.4 14.4 %all-to-all-start = ((bf16[64,4,128]{2,1,0:T(4,128)(2,1)}), bf16[64,4,128]{2,1,0:T(4,128)(2,1)S(1)}, u32[]{:S(2)}, u32[]{:S(2)}) async-start(bf16[64,4,128]{2,1,0:T(4,128)(2,1)} %broadcast_select_fusion.2), calls=%async_computation | async-start | bytes 131072 | tf_op jit(solution)/shard_map/while/body/eval_jaxpr/all_to_all | solution.py:65
  146.9 6.3 %collective-permute-start = (bf16[128,1]{1,0:T(8,128)(2,1)S(1)}, bf16[128,1]{1,0:T(8,128)(2,1)S(1)}, u32[]{:S(2)}, u32[]{:S(2)}) collective-permute-start(bf16[128,1]{1,0:T(8,128)(2,1)S(1)} %get-tuple-element.170), channel_id=1, source_target_pairs={{1,0},{2,1},{3,2},{5,4},{6,5},{7,6},{9,8},{10,9},{11,10},{13,12},{... | collective-permute-start | bytes 776 | tf_op jit(solution)/shard_map/while/body/eval_jaxpr/ppermute | solution.py:19
  148.2 6.4 %collective-permute-start.1 = (bf16[128,1]{1,0:T(8,128)(2,1)S(1)}, bf16[128,1]{1,0:T(8,128)(2,1)S(1)}, u32[]{:S(2)}, u32[]{:S(2)}) collective-permute-start(bf16[128,1]{1,0:T(8,128)(2,1)S(1)} %get-tuple-element.171), channel_id=1, source_target_pairs={{0,1},{1,2},{2,3},{4,5},{5,6},{6,7},{8,9},{9,10},{10,11},{12,13},{... | collective-permute-start | bytes 776 | tf_op jit(solution)/shard_map/while/body/eval_jaxpr/ppermute | solution.py:16
  157.7 14.4 %all-to-all-start = ((bf16[64,4,128]{2,1,0:T(4,128)(2,1)}), bf16[64,4,128]{2,1,0:T(4,128)(2,1)S(1)}, u32[]{:S(2)}, u32[]{:S(2)}) async-start(bf16[64,4,128]{2,1,0:T(4,128)(2,1)} %broadcast_select_fusion.2), calls=%async_computation | async-start | bytes 131072 | tf_op jit(solution)/shard_map/while/body/eval_jaxpr/all_to_all | solution.py:65
  172.2 6.3 %collective-permute-start = (bf16[128,1]{1,0:T(8,128)(2,1)S(1)}, bf16[128,1]{1,0:T(8,128)(2,1)S(1)}, u32[]{:S(2)}, u32[]{:S(2)}) collective-permute-start(bf16[128,1]{1,0:T(8,128)(2,1)S(1)} %get-tuple-element.170), channel_id=1, source_target_pairs={{1,0},{2,1},{3,2},{5,4},{6,5},{7,6},{9,8},{10,9},{11,10},{13,12},{... | collective-permute-start | bytes 776 | tf_op jit(solution)/shard_map/while/body/eval_jaxpr/ppermute | solution.py:19
  173.5 6.4 %collective-permute-start.1 = (bf16[128,1]{1,0:T(8,128)(2,1)S(1)}, bf16[128,1]{1,0:T(8,128)(2,1)S(1)}, u32[]{:S(2)}, u32[]{:S(2)}) collective-permute-start(bf16[128,1]{1,0:T(8,128)(2,1)S(1)} %get-tuple-element.171), channel_id=1, source_target_pairs={{0,1},{1,2},{2,3},{4,5},{5,6},{6,7},{8,9},{9,10},{10,11},{12,13},{... | collective-permute-start | bytes 776 | tf_op jit(solution)/shard_map/while/body/eval_jaxpr/ppermute | solution.py:16
  182.9 14.4 %all-to-all-start = ((bf16[64,4,128]{2,1,0:T(4,128)(2,1)}), bf16[64,4,128]{2,1,0:T(4,128)(2,1)S(1)}, u32[]{:S(2)}, u32[]{:S(2)}) async-start(bf16[64,4,128]{2,1,0:T(4,128)(2,1)} %broadcast_select_fusion.2), calls=%async_computation | async-start | bytes 131072 | tf_op jit(solution)/shard_map/while/body/eval_jaxpr/all_to_all | solution.py:65
  197.5 6.3 %collective-permute-start = (bf16[128,1]{1,0:T(8,128)(2,1)S(1)}, bf16[128,1]{1,0:T(8,128)(2,1)S(1)}, u32[]{:S(2)}, u32[]{:S(2)}) collective-permute-start(bf16[128,1]{1,0:T(8,128)(2,1)S(1)} %get-tuple-element.170), channel_id=1, source_target_pairs={{1,0},{2,1},{3,2},{5,4},{6,5},{7,6},{9,8},{10,9},{11,10},{13,12},{... | collective-permute-start | bytes 776 | tf_op jit(solution)/shard_map/while/body/eval_jaxpr/ppermute | solution.py:19
  198.7 6.4 %collective-permute-start.1 = (bf16[128,1]{1,0:T(8,128)(2,1)S(1)}, bf16[128,1]{1,0:T(8,128)(2,1)S(1)}, u32[]{:S(2)}, u32[]{:S(2)}) collective-permute-start(bf16[128,1]{1,0:T(8,128)(2,1)S(1)} %get-tuple-element.171), channel_id=1, source_target_pairs={{0,1},{1,2},{2,3},{4,5},{5,6},{6,7},{8,9},{9,10},{10,11},{12,13},{... | collective-permute-start | bytes 776 | tf_op jit(solution)/shard_map/while/body/eval_jaxpr/ppermute | solution.py:16
  208.2 14.4 %all-to-all-start = ((bf16[64,4,128]{2,1,0:T(4,128)(2,1)}), bf16[64,4,128]{2,1,0:T(4,128)(2,1)S(1)}, u32[]{:S(2)}, u32[]{:S(2)}) async-start(bf16[64,4,128]{2,1,0:T(4,128)(2,1)} %broadcast_select_fusion.2), calls=%async_computation | async-start | bytes 131072 | tf_op jit(solution)/shard_map/while/body/eval_jaxpr/all_to_all | solution.py:65
  222.6 248.6 %copy-start = (f32[128,128]{1,0:T(8,128)}, f32[128,128]{1,0:T(8,128)S(1)}, u32[]{:S(2)}) copy-start(f32[128,128]{1,0:T(8,128)S(1)} %get-tuple-element.81) | copy-start | bytes 196612
  222.6 6.0 %copy-start.1 = (s32[1,128,2]{1,2,0:T(2,128)S(1)}, s32[1,128,2]{1,2,0:T(2,128)}, u32[]{:S(2)}) copy-start(s32[1,128,2]{1,2,0:T(2,128)} %param.18) | copy-start | bytes 3076
Sparse Core Ops, SparseCore 0:
  230.2 239.5 all-reduce.2
where the time goes:
time: 480 us; the launch traced here: 478 us
  waiting for transfers between devices  322 us (67%)
  starting transfers between devices  99.5 us (21%)
  matrix products  15.6 us (3%)
  local copies, waits for them, and re-layouts  14.6 us (3%)
  between operations  14.1 us (3%)
  other arithmetic  11.6 us (2%)
    psum x1, waiting for transfers between devices, on_device(): summed = lax.psum(partial_sum, ('tile', 'sec'))  240 us
    all_to_all x8, waiting for transfers between devices, advance_send(): lax.all_to_all(outgoing, 'tile', split_axis=0, concat_axis=0, tiled=True)  70.7 us
    all_to_all x8, starting transfers between devices, advance_send(): lax.all_to_all(outgoing, 'tile', split_axis=0, concat_axis=0, tiled=True)  50.7 us
    ppermute x8, starting transfers between devices, padded_2(): lax.ppermute(lax.slice_in_dim(block, block.shape[dim] - width, None, axis...  38.5 us
    ppermute x8, waiting for transfers between devices, padded_2(): lax.ppermute(lax.slice_in_dim(block, block.shape[dim] - width, None, axis...  11.2 us
    ppermute x8, starting transfers between devices, padded_2(): lax.ppermute(lax.slice_in_dim(block, 0, width, axis=dim), axis, backward)  10.3 us
    dot_general x8, matrix products, cable_update(): jnp.einsum('ci,ji->cj', right_side, inv_cable, precision=lax.Precision.HI...  10.2 us
  transfers between devices with their start and end apart: 25, of which 17 were waited for; matrix products, arithmetic and copies ran while one was open for 0% of the time, Pallas kernels for 0%

commit v1 on v0

--- a/solution.py
+++ b/solution.py
@@ -85,7 +85,7 @@
     )
     partial_sum = jnp.einsum("tskc,skq->tqc", tile_sums, select, precision=lax.Precision.HIGHEST)
     partial_sum = partial_sum.reshape(step_count, tile_total * contact_width)
-    summed = lax.psum(partial_sum, ("tile", "sec"))
+    summed = jnp.sum(lax.all_gather(partial_sum, ("tile", "sec")), axis=0)
     share_width = summed.shape[1] // (tile_count * section_count)
     position = lax.axis_index("tile") * section_count + lax.axis_index("sec")
     probe_share = lax.dynamic_slice_in_dim(summed, position * share_width, share_width, 1)

time: 480 us -> 403 us (0.84)
  waiting for transfers between devices: 322 us -> 232 us
  other arithmetic: 11.6 us -> 23.7 us
    psum x1 -> x0, waiting for transfers between devices: 240 us -> none  [on_device(): summed = lax.psum(partial_sum, ('tile', 'sec'))]
    all_gather x0 -> x1, waiting for transfers between devices: none -> 150 us  [on_device(): summed = jnp.sum(lax.all_gather(partial_sum, ('tile', 'sec')), axis=0)]
    reduce_sum x0 -> x1, other arithmetic: none -> 12.1 us  [on_device(): summed = jnp.sum(lax.all_gather(partial_sum, ('tile', 'sec')), axis=0)]
where the time goes in v1:
time: 403 us; the launch traced here: 400 us
  waiting for transfers between devices  232 us (58%)
  starting transfers between devices  99.4 us (25%)
  other arithmetic  23.7 us (6%)
  matrix products  15.6 us (4%)
  between operations  14.1 us (3%)
  local copies, waits for them, and re-layouts  13.9 us (3%)
    all_gather x1, waiting for transfers between devices, on_device(): summed = jnp.sum(lax.all_gather(partial_sum, ('tile', 'sec')), axis=0)  150 us
    all_to_all x8, waiting for transfers between devices, advance_send(): lax.all_to_all(outgoing, 'tile', split_axis=0, concat_axis=0, tiled=True)  70.7 us
    all_to_all x8, starting transfers between devices, advance_send(): lax.all_to_all(outgoing, 'tile', split_axis=0, concat_axis=0, tiled=True)  50.6 us
    ppermute x8, starting transfers between devices, padded_2(): lax.ppermute(lax.slice_in_dim(block, block.shape[dim] - width, None, axis...  38.5 us
    reduce_sum x1, other arithmetic, on_device(): summed = jnp.sum(lax.all_gather(partial_sum, ('tile', 'sec')), axis=0)  12.1 us
    ppermute x8, waiting for transfers between devices, padded_2(): lax.ppermute(lax.slice_in_dim(block, block.shape[dim] - width, None, axis...  11.2 us
    ppermute x8, starting transfers between devices, padded_2(): lax.ppermute(lax.slice_in_dim(block, 0, width, axis=dim), axis, backward)  10.3 us
    dot_general x8, matrix products, cable_update(): jnp.einsum('ci,ji->cj', right_side, inv_cable, precision=lax.Precision.HI...  10.2 us
  transfers between devices with their start and end apart: 25, of which 17 were waited for; matrix products, arithmetic and copies ran while one was open for 0% of the time, Pallas kernels for 0%

profile of v1, /device:TPU:8, one launch (start us, length us, event | category | flops | bytes accessed | tf_op | source)
XLA Modules:
  0.0 399.7 jit_solution(3590270890387293496)
XLA Ops:
  14.3 208.3 %while.13 = (s32[]{:T(128)}, f32[128,128]{1,0:T(8,128)S(1)}, bf16[8,64,4,128]{3,2,1,0:T(4,128)(2,1)S(1)}, f32[128,128]{1,0:T(8,128)}, bf16[8,128,128]{2,1,0:T(8,...) while((s32[]{:T(128)}, f32[128,128]{1,0:T(8,128)S(1)}, ...), condition=%wide.region_4.5_spmd, body=%wide.region_3.4_spmd.sunk | while | flops 25629952 | bytes 1626603 | solution.py:68
  14.4 1.3 collective-permute-start
  15.7 4.5 %collective-permute-start.1 = (bf16[128,1]{1,0:T(8,128)(2,1)S(1)}, bf16[128,1]{1,0:T(8,128)(2,1)S(1)}, u32[]{:S(2)}, u32[]{:S(2)}) collective-permute-start(bf16[128,1]{1,0:T(8,128)(2,1)S(1)} %get-tuple-element.171), channel_id=1, source_target_pairs={{0,1},{1,2},{2,3},{4,5},{5,6},{6,7},{8,9},{9,10},{10,11},{12,13},{... | collective-permute-start | bytes 776 | tf_op jit(solution)/shard_map/while/body/eval_jaxpr/ppermute | solution.py:16
  20.4 1.4 collective-permute-done.1
  24.8 12.1 %all-to-all-start = ((bf16[64,4,128]{2,1,0:T(4,128)(2,1)}), bf16[64,4,128]{2,1,0:T(4,128)(2,1)S(1)}, u32[]{:S(2)}, u32[]{:S(2)}) async-start(bf16[64,4,128]{2,1,0:T(4,128)(2,1)} %broadcast_select_fusion.2), calls=%async_computation | async-start | bytes 131072 | tf_op jit(solution)/shard_map/while/body/eval_jaxpr/all_to_all | solution.py:65
  36.9 8.8 %all-to-all-done = bf16[64,4,128]{2,1,0:T(4,128)(2,1)S(1)} async-done(((bf16[64,4,128]{2,1,0:T(4,128)(2,1)}), bf16[64,4,128]{2,1,0:T(4,128)(2,1)S(1)}, u32[]{:S(2)}, u32[]{:S(2)}) %all-to-all-start) | async-done | bytes 65568 | tf_op jit(solution)/shard_map/while/body/eval_jaxpr/all_to_all | solution.py:65
  45.9 1.3 collective-permute-start
  47.2 4.9 %collective-permute-start.1 = (bf16[128,1]{1,0:T(8,128)(2,1)S(1)}, bf16[128,1]{1,0:T(8,128)(2,1)S(1)}, u32[]{:S(2)}, u32[]{:S(2)}) collective-permute-start(bf16[128,1]{1,0:T(8,128)(2,1)S(1)} %get-tuple-element.171), channel_id=1, source_target_pairs={{0,1},{1,2},{2,3},{4,5},{5,6},{6,7},{8,9},{9,10},{10,11},{12,13},{... | collective-permute-start | bytes 776 | tf_op jit(solution)/shard_map/while/body/eval_jaxpr/ppermute | solution.py:16
  52.2 1.4 collective-permute-done.1
  56.7 5.5 %all-to-all-start = ((bf16[64,4,128]{2,1,0:T(4,128)(2,1)}), bf16[64,4,128]{2,1,0:T(4,128)(2,1)S(1)}, u32[]{:S(2)}, u32[]{:S(2)}) async-start(bf16[64,4,128]{2,1,0:T(4,128)(2,1)} %broadcast_select_fusion.2), calls=%async_computation | async-start | bytes 131072 | tf_op jit(solution)/shard_map/while/body/eval_jaxpr/all_to_all | solution.py:65
  62.2 8.8 %all-to-all-done = bf16[64,4,128]{2,1,0:T(4,128)(2,1)S(1)} async-done(((bf16[64,4,128]{2,1,0:T(4,128)(2,1)}), bf16[64,4,128]{2,1,0:T(4,128)(2,1)S(1)}, u32[]{:S(2)}, u32[]{:S(2)}) %all-to-all-start) | async-done | bytes 65568 | tf_op jit(solution)/shard_map/while/body/eval_jaxpr/all_to_all | solution.py:65
  71.2 1.3 collective-permute-start
  72.5 4.9 %collective-permute-start.1 = (bf16[128,1]{1,0:T(8,128)(2,1)S(1)}, bf16[128,1]{1,0:T(8,128)(2,1)S(1)}, u32[]{:S(2)}, u32[]{:S(2)}) collective-permute-start(bf16[128,1]{1,0:T(8,128)(2,1)S(1)} %get-tuple-element.171), channel_id=1, source_target_pairs={{0,1},{1,2},{2,3},{4,5},{5,6},{6,7},{8,9},{9,10},{10,11},{12,13},{... | collective-permute-start | bytes 776 | tf_op jit(solution)/shard_map/while/body/eval_jaxpr/ppermute | solution.py:16
  77.5 1.4 collective-permute-done.1
  79.0 1.3 fusion.52
  81.9 5.5 %all-to-all-start = ((bf16[64,4,128]{2,1,0:T(4,128)(2,1)}), bf16[64,4,128]{2,1,0:T(4,128)(2,1)S(1)}, u32[]{:S(2)}, u32[]{:S(2)}) async-start(bf16[64,4,128]{2,1,0:T(4,128)(2,1)} %broadcast_select_fusion.2), calls=%async_computation | async-start | bytes 131072 | tf_op jit(solution)/shard_map/while/body/eval_jaxpr/all_to_all | solution.py:65
  87.4 8.8 %all-to-all-done = bf16[64,4,128]{2,1,0:T(4,128)(2,1)S(1)} async-done(((bf16[64,4,128]{2,1,0:T(4,128)(2,1)}), bf16[64,4,128]{2,1,0:T(4,128)(2,1)S(1)}, u32[]{:S(2)}, u32[]{:S(2)}) %all-to-all-start) | async-done | bytes 65568 | tf_op jit(solution)/shard_map/while/body/eval_jaxpr/all_to_all | solution.py:65
  96.4 1.3 collective-permute-start
  97.7 4.9 %collective-permute-start.1 = (bf16[128,1]{1,0:T(8,128)(2,1)S(1)}, bf16[128,1]{1,0:T(8,128)(2,1)S(1)}, u32[]{:S(2)}, u32[]{:S(2)}) collective-permute-start(bf16[128,1]{1,0:T(8,128)(2,1)S(1)} %get-tuple-element.171), channel_id=1, source_target_pairs={{0,1},{1,2},{2,3},{4,5},{5,6},{6,7},{8,9},{9,10},{10,11},{12,13},{... | collective-permute-start | bytes 776 | tf_op jit(solution)/shard_map/while/body/eval_jaxpr/ppermute | solution.py:16
  102.8 1.4 collective-permute-done.1
  104.3 1.3 fusion.52
  107.2 5.5 %all-to-all-start = ((bf16[64,4,128]{2,1,0:T(4,128)(2,1)}), bf16[64,4,128]{2,1,0:T(4,128)(2,1)S(1)}, u32[]{:S(2)}, u32[]{:S(2)}) async-start(bf16[64,4,128]{2,1,0:T(4,128)(2,1)} %broadcast_select_fusion.2), calls=%async_computation | async-start | bytes 131072 | tf_op jit(solution)/shard_map/while/body/eval_jaxpr/all_to_all | solution.py:65
  112.7 8.8 %all-to-all-done = bf16[64,4,128]{2,1,0:T(4,128)(2,1)S(1)} async-done(((bf16[64,4,128]{2,1,0:T(4,128)(2,1)}), bf16[64,4,128]{2,1,0:T(4,128)(2,1)S(1)}, u32[]{:S(2)}, u32[]{:S(2)}) %all-to-all-start) | async-done | bytes 65568 | tf_op jit(solution)/shard_map/while/body/eval_jaxpr/all_to_all | solution.py:65
  121.7 1.3 collective-permute-start
  123.0 4.8 %collective-permute-start.1 = (bf16[128,1]{1,0:T(8,128)(2,1)S(1)}, bf16[128,1]{1,0:T(8,128)(2,1)S(1)}, u32[]{:S(2)}, u32[]{:S(2)}) collective-permute-start(bf16[128,1]{1,0:T(8,128)(2,1)S(1)} %get-tuple-element.171), channel_id=1, source_target_pairs={{0,1},{1,2},{2,3},{4,5},{5,6},{6,7},{8,9},{9,10},{10,11},{12,13},{... | collective-permute-start | bytes 776 | tf_op jit(solution)/shard_map/while/body/eval_jaxpr/ppermute | solution.py:16
  128.0 1.4 collective-permute-done.1
  132.4 5.5 %all-to-all-start = ((bf16[64,4,128]{2,1,0:T(4,128)(2,1)}), bf16[64,4,128]{2,1,0:T(4,128)(2,1)S(1)}, u32[]{:S(2)}, u32[]{:S(2)}) async-start(bf16[64,4,128]{2,1,0:T(4,128)(2,1)} %broadcast_select_fusion.2), calls=%async_computation | async-start | bytes 131072 | tf_op jit(solution)/shard_map/while/body/eval_jaxpr/all_to_all | solution.py:65
  137.9 8.8 %all-to-all-done = bf16[64,4,128]{2,1,0:T(4,128)(2,1)S(1)} async-done(((bf16[64,4,128]{2,1,0:T(4,128)(2,1)}), bf16[64,4,128]{2,1,0:T(4,128)(2,1)S(1)}, u32[]{:S(2)}, u32[]{:S(2)}) %all-to-all-start) | async-done | bytes 65568 | tf_op jit(solution)/shard_map/while/body/eval_jaxpr/all_to_all | solution.py:65
  146.9 1.3 collective-permute-start
  148.2 4.9 %collective-permute-start.1 = (bf16[128,1]{1,0:T(8,128)(2,1)S(1)}, bf16[128,1]{1,0:T(8,128)(2,1)S(1)}, u32[]{:S(2)}, u32[]{:S(2)}) collective-permute-start(bf16[128,1]{1,0:T(8,128)(2,1)S(1)} %get-tuple-element.171), channel_id=1, source_target_pairs={{0,1},{1,2},{2,3},{4,5},{5,6},{6,7},{8,9},{9,10},{10,11},{12,13},{... | collective-permute-start | bytes 776 | tf_op jit(solution)/shard_map/while/body/eval_jaxpr/ppermute | solution.py:16
  153.3 1.4 collective-permute-done.1
  154.8 1.3 fusion.52
  157.7 5.5 %all-to-all-start = ((bf16[64,4,128]{2,1,0:T(4,128)(2,1)}), bf16[64,4,128]{2,1,0:T(4,128)(2,1)S(1)}, u32[]{:S(2)}, u32[]{:S(2)}) async-start(bf16[64,4,128]{2,1,0:T(4,128)(2,1)} %broadcast_select_fusion.2), calls=%async_computation | async-start | bytes 131072 | tf_op jit(solution)/shard_map/while/body/eval_jaxpr/all_to_all | solution.py:65
  163.2 8.8 %all-to-all-done = bf16[64,4,128]{2,1,0:T(4,128)(2,1)S(1)} async-done(((bf16[64,4,128]{2,1,0:T(4,128)(2,1)}), bf16[64,4,128]{2,1,0:T(4,128)(2,1)S(1)}, u32[]{:S(2)}, u32[]{:S(2)}) %all-to-all-start) | async-done | bytes 65568 | tf_op jit(solution)/shard_map/while/body/eval_jaxpr/all_to_all | solution.py:65
  172.2 1.3 collective-permute-start
  173.5 4.8 %collective-permute-start.1 = (bf16[128,1]{1,0:T(8,128)(2,1)S(1)}, bf16[128,1]{1,0:T(8,128)(2,1)S(1)}, u32[]{:S(2)}, u32[]{:S(2)}) collective-permute-start(bf16[128,1]{1,0:T(8,128)(2,1)S(1)} %get-tuple-element.171), channel_id=1, source_target_pairs={{0,1},{1,2},{2,3},{4,5},{5,6},{6,7},{8,9},{9,10},{10,11},{12,13},{... | collective-permute-start | bytes 776 | tf_op jit(solution)/shard_map/while/body/eval_jaxpr/ppermute | solution.py:16
  178.5 1.4 collective-permute-done.1
  182.9 5.5 %all-to-all-start = ((bf16[64,4,128]{2,1,0:T(4,128)(2,1)}), bf16[64,4,128]{2,1,0:T(4,128)(2,1)S(1)}, u32[]{:S(2)}, u32[]{:S(2)}) async-start(bf16[64,4,128]{2,1,0:T(4,128)(2,1)} %broadcast_select_fusion.2), calls=%async_computation | async-start | bytes 131072 | tf_op jit(solution)/shard_map/while/body/eval_jaxpr/all_to_all | solution.py:65
  188.4 8.8 %all-to-all-done = bf16[64,4,128]{2,1,0:T(4,128)(2,1)S(1)} async-done(((bf16[64,4,128]{2,1,0:T(4,128)(2,1)}), bf16[64,4,128]{2,1,0:T(4,128)(2,1)S(1)}, u32[]{:S(2)}, u32[]{:S(2)}) %all-to-all-start) | async-done | bytes 65568 | tf_op jit(solution)/shard_map/while/body/eval_jaxpr/all_to_all | solution.py:65
  197.4 1.3 collective-permute-start
  198.7 4.9 %collective-permute-start.1 = (bf16[128,1]{1,0:T(8,128)(2,1)S(1)}, bf16[128,1]{1,0:T(8,128)(2,1)S(1)}, u32[]{:S(2)}, u32[]{:S(2)}) collective-permute-start(bf16[128,1]{1,0:T(8,128)(2,1)S(1)} %get-tuple-element.171), channel_id=1, source_target_pairs={{0,1},{1,2},{2,3},{4,5},{5,6},{6,7},{8,9},{9,10},{10,11},{12,13},{... | collective-permute-start | bytes 776 | tf_op jit(solution)/shard_map/while/body/eval_jaxpr/ppermute | solution.py:16
  203.8 1.4 collective-permute-done.1
  205.3 1.3 fusion.52
  208.2 5.5 %all-to-all-start = ((bf16[64,4,128]{2,1,0:T(4,128)(2,1)}), bf16[64,4,128]{2,1,0:T(4,128)(2,1)S(1)}, u32[]{:S(2)}, u32[]{:S(2)}) async-start(bf16[64,4,128]{2,1,0:T(4,128)(2,1)} %broadcast_select_fusion.2), calls=%async_computation | async-start | bytes 131072 | tf_op jit(solution)/shard_map/while/body/eval_jaxpr/all_to_all | solution.py:65
  213.7 8.8 %all-to-all-done = bf16[64,4,128]{2,1,0:T(4,128)(2,1)S(1)} async-done(((bf16[64,4,128]{2,1,0:T(4,128)(2,1)}), bf16[64,4,128]{2,1,0:T(4,128)(2,1)S(1)}, u32[]{:S(2)}, u32[]{:S(2)}) %all-to-all-start) | async-done | bytes 65568 | tf_op jit(solution)/shard_map/while/body/eval_jaxpr/all_to_all | solution.py:65
  223.9 4.6 %fusion.28 = f32[8,128,2,128]{3,0,2,1:T(8,128)S(1)} fusion(bf16[1,128,2,128,128]{4,3,2,1,0:T(8,128)(2,1)} %param.19, bf16[128,8,128]{2,1,0:T(8,128)(2,1)S(1)} %gather_fusion.1, pred[128]{0:T(512)(128)(4,1)S(1)} %compare_and_fusion.1), kind=kOutput, calls=%fused_computation.41 | convolution fusion | flops 67239936 | bytes 9699456 | tf_op jit(solution)/shard_map/tsi,skic->tskc/dot_general | solution.py:82
  230.0 150.1 %all-gather.2.cloned.1.call-done = f32[256,8,4096]{2,1,0:T(8,128)} async-done(((f32[1,8,4096]{2,1,0:T(8,128)}), f32[256,8,4096]{2,1,0:T(8,128)}) %all-gather.2.cloned.1.call-update) | async-done | bytes 33554448 | tf_op jit(solution)/shard_map/all_gather | solution.py:88
  380.1 12.1 %reduce_sum.42 = f32[8,4096]{1,0:T(8,128)S(1)} reduce(f32[256,8,4096]{2,1,0:T(8,128)} %all-gather.2.cloned.1.call-done, f32[]{:T(128)} %constant.92.clone.1), dimensions={0}, to_apply=%region_8.9 | reduce | flops 8355840 | bytes 33685508 | tf_op jit(solution)/shard_map/reduce_sum | solution.py:88
  (145 shorter events, 31.4 us)
Async XLA Ops:
  7.2 373.0 %all-gather.2.cloned.1.call-start = ((), (), s32[]{:S(2)}) async-start(), calls=%async_computation.1 | async-start | bytes 33685504 | tf_op jit(solution)/shard_map/all_gather | solution.py:88
  14.4 6.0 %collective-permute-start = (bf16[128,1]{1,0:T(8,128)(2,1)S(1)}, bf16[128,1]{1,0:T(8,128)(2,1)S(1)}, u32[]{:S(2)}, u32[]{:S(2)}) collective-permute-start(bf16[128,1]{1,0:T(8,128)(2,1)S(1)} %get-tuple-element.170), channel_id=1, source_target_pairs={{1,0},{2,1},{3,2},{5,4},{6,5},{7,6},{9,8},{10,9},{11,10},{13,12},{... | collective-permute-start | bytes 776 | tf_op jit(solution)/shard_map/while/body/eval_jaxpr/ppermute | solution.py:19
  15.7 6.1 %collective-permute-start.1 = (bf16[128,1]{1,0:T(8,128)(2,1)S(1)}, bf16[128,1]{1,0:T(8,128)(2,1)S(1)}, u32[]{:S(2)}, u32[]{:S(2)}) collective-permute-start(bf16[128,1]{1,0:T(8,128)(2,1)S(1)} %get-tuple-element.171), channel_id=1, source_target_pairs={{0,1},{1,2},{2,3},{4,5},{5,6},{6,7},{8,9},{9,10},{10,11},{12,13},{... | collective-permute-start | bytes 776 | tf_op jit(solution)/shard_map/while/body/eval_jaxpr/ppermute | solution.py:16
  24.8 20.9 %all-to-all-start = ((bf16[64,4,128]{2,1,0:T(4,128)(2,1)}), bf16[64,4,128]{2,1,0:T(4,128)(2,1)S(1)}, u32[]{:S(2)}, u32[]{:S(2)}) async-start(bf16[64,4,128]{2,1,0:T(4,128)(2,1)} %broadcast_select_fusion.2), calls=%async_computation | async-start | bytes 131072 | tf_op jit(solution)/shard_map/while/body/eval_jaxpr/all_to_all | solution.py:65
  45.9 6.3 %collective-permute-start = (bf16[128,1]{1,0:T(8,128)(2,1)S(1)}, bf16[128,1]{1,0:T(8,128)(2,1)S(1)}, u32[]{:S(2)}, u32[]{:S(2)}) collective-permute-start(bf16[128,1]{1,0:T(8,128)(2,1)S(1)} %get-tuple-element.170), channel_id=1, source_target_pairs={{1,0},{2,1},{3,2},{5,4},{6,5},{7,6},{9,8},{10,9},{11,10},{13,12},{... | collective-permute-start | bytes 776 | tf_op jit(solution)/shard_map/while/body/eval_jaxpr/ppermute | solution.py:19
  47.2 6.4 %collective-permute-start.1 = (bf16[128,1]{1,0:T(8,128)(2,1)S(1)}, bf16[128,1]{1,0:T(8,128)(2,1)S(1)}, u32[]{:S(2)}, u32[]{:S(2)}) collective-permute-start(bf16[128,1]{1,0:T(8,128)(2,1)S(1)} %get-tuple-element.171), channel_id=1, source_target_pairs={{0,1},{1,2},{2,3},{4,5},{5,6},{6,7},{8,9},{9,10},{10,11},{12,13},{... | collective-permute-start | bytes 776 | tf_op jit(solution)/shard_map/while/body/eval_jaxpr/ppermute | solution.py:16
  56.7 14.3 %all-to-all-start = ((bf16[64,4,128]{2,1,0:T(4,128)(2,1)}), bf16[64,4,128]{2,1,0:T(4,128)(2,1)S(1)}, u32[]{:S(2)}, u32[]{:S(2)}) async-start(bf16[64,4,128]{2,1,0:T(4,128)(2,1)} %broadcast_select_fusion.2), calls=%async_computation | async-start | bytes 131072 | tf_op jit(solution)/shard_map/while/body/eval_jaxpr/all_to_all | solution.py:65
  71.2 6.3 %collective-permute-start = (bf16[128,1]{1,0:T(8,128)(2,1)S(1)}, bf16[128,1]{1,0:T(8,128)(2,1)S(1)}, u32[]{:S(2)}, u32[]{:S(2)}) collective-permute-start(bf16[128,1]{1,0:T(8,128)(2,1)S(1)} %get-tuple-element.170), channel_id=1, source_target_pairs={{1,0},{2,1},{3,2},{5,4},{6,5},{7,6},{9,8},{10,9},{11,10},{13,12},{... | collective-permute-start | bytes 776 | tf_op jit(solution)/shard_map/while/body/eval_jaxpr/ppermute | solution.py:19
  72.5 6.4 %collective-permute-start.1 = (bf16[128,1]{1,0:T(8,128)(2,1)S(1)}, bf16[128,1]{1,0:T(8,128)(2,1)S(1)}, u32[]{:S(2)}, u32[]{:S(2)}) collective-permute-start(bf16[128,1]{1,0:T(8,128)(2,1)S(1)} %get-tuple-element.171), channel_id=1, source_target_pairs={{0,1},{1,2},{2,3},{4,5},{5,6},{6,7},{8,9},{9,10},{10,11},{12,13},{... | collective-permute-start | bytes 776 | tf_op jit(solution)/shard_map/while/body/eval_jaxpr/ppermute | solution.py:16
  81.9 14.3 %all-to-all-start = ((bf16[64,4,128]{2,1,0:T(4,128)(2,1)}), bf16[64,4,128]{2,1,0:T(4,128)(2,1)S(1)}, u32[]{:S(2)}, u32[]{:S(2)}) async-start(bf16[64,4,128]{2,1,0:T(4,128)(2,1)} %broadcast_select_fusion.2), calls=%async_computation | async-start | bytes 131072 | tf_op jit(solution)/shard_map/while/body/eval_jaxpr/all_to_all | solution.py:65
  96.4 6.3 %collective-permute-start = (bf16[128,1]{1,0:T(8,128)(2,1)S(1)}, bf16[128,1]{1,0:T(8,128)(2,1)S(1)}, u32[]{:S(2)}, u32[]{:S(2)}) collective-permute-start(bf16[128,1]{1,0:T(8,128)(2,1)S(1)} %get-tuple-element.170), channel_id=1, source_target_pairs={{1,0},{2,1},{3,2},{5,4},{6,5},{7,6},{9,8},{10,9},{11,10},{13,12},{... | collective-permute-start | bytes 776 | tf_op jit(solution)/shard_map/while/body/eval_jaxpr/ppermute | solution.py:19
  97.7 6.4 %collective-permute-start.1 = (bf16[128,1]{1,0:T(8,128)(2,1)S(1)}, bf16[128,1]{1,0:T(8,128)(2,1)S(1)}, u32[]{:S(2)}, u32[]{:S(2)}) collective-permute-start(bf16[128,1]{1,0:T(8,128)(2,1)S(1)} %get-tuple-element.171), channel_id=1, source_target_pairs={{0,1},{1,2},{2,3},{4,5},{5,6},{6,7},{8,9},{9,10},{10,11},{12,13},{... | collective-permute-start | bytes 776 | tf_op jit(solution)/shard_map/while/body/eval_jaxpr/ppermute | solution.py:16
  107.2 14.4 %all-to-all-start = ((bf16[64,4,128]{2,1,0:T(4,128)(2,1)}), bf16[64,4,128]{2,1,0:T(4,128)(2,1)S(1)}, u32[]{:S(2)}, u32[]{:S(2)}) async-start(bf16[64,4,128]{2,1,0:T(4,128)(2,1)} %broadcast_select_fusion.2), calls=%async_computation | async-start | bytes 131072 | tf_op jit(solution)/shard_map/while/body/eval_jaxpr/all_to_all | solution.py:65
  121.7 6.3 %collective-permute-start = (bf16[128,1]{1,0:T(8,128)(2,1)S(1)}, bf16[128,1]{1,0:T(8,128)(2,1)S(1)}, u32[]{:S(2)}, u32[]{:S(2)}) collective-permute-start(bf16[128,1]{1,0:T(8,128)(2,1)S(1)} %get-tuple-element.170), channel_id=1, source_target_pairs={{1,0},{2,1},{3,2},{5,4},{6,5},{7,6},{9,8},{10,9},{11,10},{13,12},{... | collective-permute-start | bytes 776 | tf_op jit(solution)/shard_map/while/body/eval_jaxpr/ppermute | solution.py:19
  123.0 6.4 %collective-permute-start.1 = (bf16[128,1]{1,0:T(8,128)(2,1)S(1)}, bf16[128,1]{1,0:T(8,128)(2,1)S(1)}, u32[]{:S(2)}, u32[]{:S(2)}) collective-permute-start(bf16[128,1]{1,0:T(8,128)(2,1)S(1)} %get-tuple-element.171), channel_id=1, source_target_pairs={{0,1},{1,2},{2,3},{4,5},{5,6},{6,7},{8,9},{9,10},{10,11},{12,13},{... | collective-permute-start | bytes 776 | tf_op jit(solution)/shard_map/while/body/eval_jaxpr/ppermute | solution.py:16
  132.4 14.3 %all-to-all-start = ((bf16[64,4,128]{2,1,0:T(4,128)(2,1)}), bf16[64,4,128]{2,1,0:T(4,128)(2,1)S(1)}, u32[]{:S(2)}, u32[]{:S(2)}) async-start(bf16[64,4,128]{2,1,0:T(4,128)(2,1)} %broadcast_select_fusion.2), calls=%async_computation | async-start | bytes 131072 | tf_op jit(solution)/shard_map/while/body/eval_jaxpr/all_to_all | solution.py:65
  146.9 6.3 %collective-permute-start = (bf16[128,1]{1,0:T(8,128)(2,1)S(1)}, bf16[128,1]{1,0:T(8,128)(2,1)S(1)}, u32[]{:S(2)}, u32[]{:S(2)}) collective-permute-start(bf16[128,1]{1,0:T(8,128)(2,1)S(1)} %get-tuple-element.170), channel_id=1, source_target_pairs={{1,0},{2,1},{3,2},{5,4},{6,5},{7,6},{9,8},{10,9},{11,10},{13,12},{... | collective-permute-start | bytes 776 | tf_op jit(solution)/shard_map/while/body/eval_jaxpr/ppermute | solution.py:19
  148.2 6.4 %collective-permute-start.1 = (bf16[128,1]{1,0:T(8,128)(2,1)S(1)}, bf16[128,1]{1,0:T(8,128)(2,1)S(1)}, u32[]{:S(2)}, u32[]{:S(2)}) collective-permute-start(bf16[128,1]{1,0:T(8,128)(2,1)S(1)} %get-tuple-element.171), channel_id=1, source_target_pairs={{0,1},{1,2},{2,3},{4,5},{5,6},{6,7},{8,9},{9,10},{10,11},{12,13},{... | collective-permute-start | bytes 776 | tf_op jit(solution)/shard_map/while/body/eval_jaxpr/ppermute | solution.py:16
  157.7 14.3 %all-to-all-start = ((bf16[64,4,128]{2,1,0:T(4,128)(2,1)}), bf16[64,4,128]{2,1,0:T(4,128)(2,1)S(1)}, u32[]{:S(2)}, u32[]{:S(2)}) async-start(bf16[64,4,128]{2,1,0:T(4,128)(2,1)} %broadcast_select_fusion.2), calls=%async_computation | async-start | bytes 131072 | tf_op jit(solution)/shard_map/while/body/eval_jaxpr/all_to_all | solution.py:65
  172.2 6.3 %collective-permute-start = (bf16[128,1]{1,0:T(8,128)(2,1)S(1)}, bf16[128,1]{1,0:T(8,128)(2,1)S(1)}, u32[]{:S(2)}, u32[]{:S(2)}) collective-permute-start(bf16[128,1]{1,0:T(8,128)(2,1)S(1)} %get-tuple-element.170), channel_id=1, source_target_pairs={{1,0},{2,1},{3,2},{5,4},{6,5},{7,6},{9,8},{10,9},{11,10},{13,12},{... | collective-permute-start | bytes 776 | tf_op jit(solution)/shard_map/while/body/eval_jaxpr/ppermute | solution.py:19
  173.5 6.4 %collective-permute-start.1 = (bf16[128,1]{1,0:T(8,128)(2,1)S(1)}, bf16[128,1]{1,0:T(8,128)(2,1)S(1)}, u32[]{:S(2)}, u32[]{:S(2)}) collective-permute-start(bf16[128,1]{1,0:T(8,128)(2,1)S(1)} %get-tuple-element.171), channel_id=1, source_target_pairs={{0,1},{1,2},{2,3},{4,5},{5,6},{6,7},{8,9},{9,10},{10,11},{12,13},{... | collective-permute-start | bytes 776 | tf_op jit(solution)/shard_map/while/body/eval_jaxpr/ppermute | solution.py:16
  182.9 14.4 %all-to-all-start = ((bf16[64,4,128]{2,1,0:T(4,128)(2,1)}), bf16[64,4,128]{2,1,0:T(4,128)(2,1)S(1)}, u32[]{:S(2)}, u32[]{:S(2)}) async-start(bf16[64,4,128]{2,1,0:T(4,128)(2,1)} %broadcast_select_fusion.2), calls=%async_computation | async-start | bytes 131072 | tf_op jit(solution)/shard_map/while/body/eval_jaxpr/all_to_all | solution.py:65
  197.4 6.3 %collective-permute-start = (bf16[128,1]{1,0:T(8,128)(2,1)S(1)}, bf16[128,1]{1,0:T(8,128)(2,1)S(1)}, u32[]{:S(2)}, u32[]{:S(2)}) collective-permute-start(bf16[128,1]{1,0:T(8,128)(2,1)S(1)} %get-tuple-element.170), channel_id=1, source_target_pairs={{1,0},{2,1},{3,2},{5,4},{6,5},{7,6},{9,8},{10,9},{11,10},{13,12},{... | collective-permute-start | bytes 776 | tf_op jit(solution)/shard_map/while/body/eval_jaxpr/ppermute | solution.py:19
  198.7 6.4 %collective-permute-start.1 = (bf16[128,1]{1,0:T(8,128)(2,1)S(1)}, bf16[128,1]{1,0:T(8,128)(2,1)S(1)}, u32[]{:S(2)}, u32[]{:S(2)}) collective-permute-start(bf16[128,1]{1,0:T(8,128)(2,1)S(1)} %get-tuple-element.171), channel_id=1, source_target_pairs={{0,1},{1,2},{2,3},{4,5},{5,6},{6,7},{8,9},{9,10},{10,11},{12,13},{... | collective-permute-start | bytes 776 | tf_op jit(solution)/shard_map/while/body/eval_jaxpr/ppermute | solution.py:16
  208.2 14.3 %all-to-all-start = ((bf16[64,4,128]{2,1,0:T(4,128)(2,1)}), bf16[64,4,128]{2,1,0:T(4,128)(2,1)S(1)}, u32[]{:S(2)}, u32[]{:S(2)}) async-start(bf16[64,4,128]{2,1,0:T(4,128)(2,1)} %broadcast_select_fusion.2), calls=%async_computation | async-start | bytes 131072 | tf_op jit(solution)/shard_map/while/body/eval_jaxpr/all_to_all | solution.py:65
  222.6 169.6 %copy-start = (f32[128,128]{1,0:T(8,128)}, f32[128,128]{1,0:T(8,128)S(1)}, u32[]{:S(2)}) copy-start(f32[128,128]{1,0:T(8,128)S(1)} %get-tuple-element.81) | copy-start | bytes 196612
  222.6 6.0 %copy-start.1 = (s32[1,128,2]{1,2,0:T(2,128)S(1)}, s32[1,128,2]{1,2,0:T(2,128)}, u32[]{:S(2)}) copy-start(s32[1,128,2]{1,2,0:T(2,128)} %param.18) | copy-start | bytes 3076
Sparse Core Ops, SparseCore 0:
  230.1 149.9 all-gather.1
